TPU v7x, 32 devices: a whole 2x2x4 slice. The times are simulated.
32 devices in a mesh: tm: 4 (over x, core), tile: 8 (over z, y).
Axes of the slice: x: 2, y: 2, z: 4, core: 2. Of those that a mesh axis runs over, the one named last changes fastest.
Arguments:
- pcs: float32 [2, 256], P(None, 'tm'), may hold values from -6 to 6
- st_eof: float32 [2, 120, 512], replicated, may hold values from -6 to 6
- spatial_eof: bfloat16 [2, 512, 64, 2048], P(None, 'tm', 'tile'), may hold values from -1 to 1
- land_sea: int32 [64, 2048], P('tile'), may hold values 0 or 1
Outputs:
- vorticity: float32 [256, 64, 2048], P('tm', 'tile')
- divergence: float32 [256, 64, 2048], P('tm', 'tile')
All inputs are finite; a program needn't handle non-finite values. No bound on the sum of `land_sea` on one device may be relied on, other than what follows from the above.
Results may differ from a plain program's by a relative error of at most 0.0041.
Values may be sent and summed in bfloat16 or wider, within the bound.
A program may use at most 128 MiB of HBM per device.

v0:
```python
import math

import jax
import jax.numpy as jnp
from jax import lax
from jax.sharding import PartitionSpec as P


def padded_2(block, sides, width):
    for axis, dim in sides:
        count = lax.axis_size(axis)
        forward = [(i, i + 1) for i in range(count - 1)]
        backward = [(target, source) for source, target in forward]
        low = lax.ppermute(
            lax.slice_in_dim(block, block.shape[dim] - width, None, axis=dim), axis, forward
        )
        high = lax.ppermute(lax.slice_in_dim(block, 0, width, axis=dim), axis, backward)
        block = jnp.concatenate([low, block, high], axis=dim)
    return block


def lagged_rc(series, st_eof, first, count):
    day_index = first + jnp.arange(count, dtype=jnp.int32)
    lag_steps = jnp.arange(st_eof.shape[1], dtype=jnp.int32)
    lag_index = day_index[:, None] - lag_steps[None, :]
    inside = lag_index >= 0
    safe_index = jnp.maximum(lag_index, 0)
    values_lag = jnp.where(inside[None], series[:, safe_index], 0.0)
    lag_total = st_eof.shape[0] * st_eof.shape[1]
    lagged = jnp.transpose(values_lag, (1, 0, 2)).reshape(count, lag_total)
    lagged_sums = jnp.dot(
        lagged,
        st_eof.reshape(lag_total, -1),
        precision=lax.Precision.HIGHEST,
        preferred_element_type=jnp.float32,
    )
    window_len = jnp.minimum(day_index + 1, st_eof.shape[1]).astype(jnp.float32)
    return lagged_sums / window_len[:, None]


def curl_div(east_pad, north_pad, latitude):
    cosine = jnp.cos(latitude)
    cos_east = east_pad * cosine[None, :, None]
    cos_north = north_pad * cosine[None, :, None]
    inner_east = east_pad[:, 1:-1]
    inner_north = north_pad[:, 1:-1]
    zonal_east = jnp.roll(inner_east, -1, axis=2) - jnp.roll(inner_east, 1, axis=2)
    zonal_north = jnp.roll(inner_north, -1, axis=2) - jnp.roll(inner_north, 1, axis=2)
    denominator = 2.0 * cosine[1:-1][None, :, None]
    vorticity = (zonal_north - (cos_east[:, 2:] - cos_east[:, :-2])) / denominator
    divergence = (zonal_east + (cos_north[:, 2:] - cos_north[:, :-2])) / denominator
    return (vorticity, divergence)


def shards(pcs, st_eof, spatial_eof, land_sea):
    day_dev = pcs.shape[1]
    all_pcs = lax.all_gather(pcs, "tm", axis=1, tiled=True)
    own_index = lax.axis_index("tm")
    lat_rows, lon_cells = land_sea.shape
    cell_count = lat_rows * lon_cells
    chan_share = spatial_eof.shape[1]
    local_eof = spatial_eof.reshape(2, chan_share, cell_count)
    own_rc = lagged_rc(all_pcs, st_eof, own_index * day_dev, day_dev).astype(jnp.bfloat16)
    fields = jnp.einsum(
        "tc,xcn->txn",
        own_rc,
        lax.all_gather(local_eof, "tm", axis=1, tiled=True),
        preferred_element_type=jnp.float32,
    )
    ocean_mask = land_sea.astype(jnp.float32)
    velocity = (
        (fields * ocean_mask.reshape(1, 1, cell_count))
        .astype(jnp.bfloat16)
        .reshape(day_dev, 2, lat_rows, lon_cells)
    )
    padded = padded_2(velocity, (("tile", 2),), 1)
    total_rows = lat_rows * lax.axis_size("tile")
    global_rows = (lax.axis_index("tile") * lat_rows).astype(jnp.float32) + jnp.arange(
        -1, lat_rows + 1, dtype=jnp.float32
    )
    latitude = (-70.0 + 140.0 * (global_rows + 0.5) / total_rows) * (math.pi / 180.0)
    vorticity, divergence = curl_div(
        padded[:, 0].astype(jnp.float32), padded[:, 1].astype(jnp.float32), latitude
    )
    return (vorticity * ocean_mask[None], divergence * ocean_mask[None])


def solution(mesh):
    return jax.shard_map(
        shards,
        mesh=mesh,
        in_specs=(P(None, "tm"), P(), P(None, "tm", "tile", None), P("tile", None)),
        out_specs=(P("tm", "tile", None), P("tm", "tile", None)),
        check_vma=False,
    )
```

profile of v0, /device:TPU:0, one launch (start us, length us, event | category | flops | bytes accessed | tf_op | source)
XLA Modules:
  0.0 354.6 jit_solution(9750223347867482415)
XLA Ops:
  7.2 0.0 copy-start
  7.2 0.0 all-gather.3.cloned.1.call-start
  7.2 13.6 %reshape.93 = bf16[2,128,16384]{2,1,0:T(8,128)(2,1)} reshape(bf16[2,128,8,2048]{3,2,1,0:T(8,128)(2,1)} %param.6) | data formatting | bytes 16777216 | tf_op jit(solution)/shard_map/reshape | solution.py:62
  20.8 0.0 copy-start.4
  20.8 0.0 all-gather.3.cloned.1.call-update
  20.8 0.0 copy-start.3
  20.8 0.1 subtract_maximum_fusion
  20.9 0.1 reshape.99
  21.0 0.4 copy-done.4
  21.5 6.0 %all-gather = f32[4,64,2]{1,2,0:T(2,128)S(1)} all-gather(f32[1,64,2]{1,2,0:T(2,128)S(1)} %bitcast.56), channel_id=1, replica_groups=mesh['tm'=4,'tile'=8] {'tm'}, dimensions={0}, use_global_device_ids=true | all-gather | bytes 2560 | tf_op jit(solution)/shard_map/all_gather | solution.py:57
  27.5 0.1 copy.8
  27.6 14.9 %gather_fusion = f32[7680,2]{1,0:T(8,128)} fusion(f32[2,256]{0,1:T(8,128)S(1)} %bitcast.54, s32[8192]{0:T(1024)S(1)} %pad_clamp_fusion), kind=kCustom, calls=%fused_computation | custom fusion | bytes 153600 | tf_op jit(solution)/shard_map/gather | solution.py:28
  42.6 3.9 %copy.9 = f32[64,120,2]{1,0,2:T(8,128)S(1)} copy(f32[64,120,2]{2,1,0:T(8,128)} %bitcast.53) | data formatting | bytes 122880 | tf_op jit(solution)/shard_map/gather | solution.py:28
  46.4 0.0 copy-done.3
  46.5 0.1 subtract_compare_fusion
  46.6 0.0 copy-done
  46.6 0.4 fusion.11
  47.0 178.2 %all-gather.3.cloned.1.call-done = bf16[2,512,16384]{2,1,0:T(8,128)(2,1)} async-done(((bf16[2,128,16384]{2,1,0:T(8,128)(2,1)}), bf16[2,512,16384]{2,1,0:T(8,128)(2,1)}) %all-gather.3.cloned.1.call-update) | async-done | bytes 33554448 | tf_op jit(solution)/shard_map/all_gather | solution.py:67
  225.2 18.5 %fusion = bf16[64,2,16384]{2,0,1:T(8,128)(2,1)} fusion(bf16[64,512,1]{1,0,2:T(8,128)(2,1)S(1)} %fusion.11, bf16[2,512,16384]{2,1,0:T(8,128)(2,1)} %all-gather.3.cloned.1.call-done, f32[16384]{0:T(1024)S(1)} %bitcast.55), kind=kOutput, calls=%fused_computation.2 | convolution fusion | flops 2151677952 | bytes 37879808 | tf_op jit(solution)/shard_map/tc,xcn->txn/dot_general | solution.py:64
  243.7 5.0 %copy.17 = bf16[16,8,8,2048]{3,2,1,0:T(8,128)(2,1)S(1)} copy(bf16[16,8,8,2048]{3,1,2,0:T(8,128)(2,1)} %bitcast.50) | data formatting | bytes 8388608
  248.7 0.0 copy-start.2
  248.7 2.0 copy-done.2
  250.7 1.4 fusion.21
  252.1 0.3 copy.14
  252.4 3.4 collective-permute-start
  255.9 0.3 copy.15
  256.2 1.5 collective-permute-start.1
  257.7 0.1 multiply_cosine_fusion
  257.7 0.1 slice_multiply_fusion
  257.8 20.9 %collective-permute-done = bf16[64,2,1,2048]{3,0,2,1:T(8,128)(2,1)S(1)} collective-permute-done((bf16[64,2,1,2048]{3,0,2,1:T(8,128)(2,1)S(1)}, bf16[64,2,1,2048]{3,0,2,1:T(8,128)(2,1)S(1)}, u32[]{:S(2)}, u32[]{:S(2)}) %collective-permute-start) | collective-permute-done | bytes 524320 | tf_op jit(solution)/shard_map/ppermute | solution.py:14
  278.6 0.8 copy.12
  279.5 0.0 collective-permute-done.1
  279.5 0.8 copy.13
  280.3 8.5 %pad_maximum_fusion = bf16[64,2,10,2048]{3,2,0,1:T(8,128)(2,1)} fusion(bf16[64,2,1,2048]{3,2,0,1:T(2,128)(2,1)S(1)} %copy.13, bf16[64,2,8,2048]{3,2,0,1:T(8,128)(2,1)} %bitcast.52, bf16[64,2,1,2048]{3,2,0,1:T(2,128)(2,1)S(1)} %copy.12), kind=kLoop, calls=%fused_computation.3 | loop fusion | flops 15728640 | bytes 10485760 | tf_op jit(solution)/shard_map/concatenate | solution.py:18
  288.8 11.3 %fusion.7 = (f32[64,10,2048]{2,1,0:T(8,128)}, f32[64,10,2048]{2,1,0:T(8,128)}) fusion(bf16[64,2,10,2048]{3,2,0,1:T(8,128)(2,1)} %pad_maximum_fusion), kind=kLoop, calls=%fused_computation.13 | loop fusion | flops 2621440 | bytes 15728640 | tf_op jit(solution)/shard_map/convert_element_type | solution.py:83
  300.1 17.3 %fusion.18 = (f32[64,8,2047]{2,1,0:T(8,128)S(1)}, f32[64,8,2047]{2,1,0:T(8,128)}, f32[64,8,2047]{2,1,0:T(8,128)}, f32[64,8,2047]{2,1,0:T(8,128)}) fusion(f32[64,10,2048]{2,1,0:T(8,128)} %get-tuple-element.8, f32[64,10,2048]{2,1,0:T(8,128)} %get-tuple-element.9), kind=kLoop, calls=%fused_computation.38 | loop fusion | bytes 33538048 | tf_op jit(solution)/shard_map/jit(_roll_static)/slice | solution.py:47
  317.5 2.6 fusion.17
  320.1 9.3 %broadcast_multiply_fusion = (f32[64,10,2048]{2,1,0:T(8,128)}, f32[64,10,2048]{2,1,0:T(8,128)}) fusion(f32[10]{0:T(128)S(1)} %multiply_cosine_fusion, bf16[64,2,10,2048]{3,2,0,1:T(8,128)(2,1)} %pad_maximum_fusion), kind=kLoop, calls=%fused_computation.18 | loop fusion | flops 5242880 | bytes 15728680 | tf_op jit(solution)/shard_map/mul | solution.py:44
  329.4 0.0 copy-start.1
  329.4 18.3 %fusion.3 = (f32[64,8,2048]{2,1,0:T(8,128)}, f32[64,8,2048]{2,1,0:T(8,128)}) fusion(f32[64,10,2048]{2,1,0:T(8,128)} %get-tuple-element.2, f32[64,8,1]{2,1,0:T(8,128)} %get-tuple-element.5, f32[64,8,2047]{2,1,0:T(8,128)} %get-tuple-element.7, f32[64,8,2047]{2,1,0:T(8,128)S(1)} %get-tuple-element.6, f32[64,8,1]{2,1,0:T(8,128)S(1)} %get-tuple-element.4, ...), kind=kLoop, calls=%fused_computation.7 | loop fusion | flops 14680064 | bytes 42008608 | tf_op jit(solution)/shard_map/mul | solution.py:85
  347.7 0.0 copy-done.1
  (5 shorter events, 0.1 us)
Async XLA Ops:
  7.2 39.4 %copy-start = (f32[2,120,512]{2,1,0:T(8,128)S(1)}, f32[2,120,512]{2,1,0:T(8,128)}, u32[]{:S(2)}) copy-start(f32[2,120,512]{2,1,0:T(8,128)} %param.5) | copy-start | bytes 1474564
  7.2 218.0 %all-gather.3.cloned.1.call-start = ((), (), s32[]{:S(2)}) async-start(), calls=%async_computation | async-start | bytes 41943040 | tf_op jit(solution)/shard_map/all_gather | solution.py:67
  20.8 0.7 copy-start.4
  20.8 25.6 %copy-start.3 = (s32[8,2048]{1,0:T(8,128)S(1)}, s32[8,2048]{1,0:T(8,128)}, u32[]{:S(2)}) copy-start(s32[8,2048]{1,0:T(8,128)} %param.7) | copy-start | bytes 196612
  248.7 2.0 copy-start.2
  252.4 26.2 %collective-permute-start = (bf16[64,2,1,2048]{3,0,2,1:T(8,128)(2,1)S(1)}, bf16[64,2,1,2048]{3,0,2,1:T(8,128)(2,1)S(1)}, u32[]{:S(2)}, u32[]{:S(2)}) collective-permute-start(bf16[64,2,1,2048]{3,0,2,1:T(8,128)(2,1)S(1)} %copy.14), channel_id=1, source_target_pairs={{0,1},{1,2},{2,3},{3,4},{4,5},{5,6},{6,7},{8,9},{9,10},{10,11},{11... | collective-permute-start | bytes 1572872 | tf_op jit(solution)/shard_map/ppermute | solution.py:14
  256.2 23.3 %collective-permute-start.1 = (bf16[64,2,1,2048]{3,0,2,1:T(8,128)(2,1)S(1)}, bf16[64,2,1,2048]{3,0,2,1:T(8,128)(2,1)S(1)}, u32[]{:S(2)}, u32[]{:S(2)}) collective-permute-start(bf16[64,2,1,2048]{3,0,2,1:T(8,128)(2,1)S(1)} %copy.15), channel_id=1, source_target_pairs={{1,0},{2,1},{3,2},{4,3},{5,4},{6,5},{7,6},{9,8},{10,9},{11,10},{12... | collective-permute-start | bytes 1572872 | tf_op jit(solution)/shard_map/ppermute | solution.py:17
  329.4 18.3 %copy-start.1 = (f32[2,120,512]{2,1,0:T(8,128)S(1)}, f32[2,120,512]{2,1,0:T(8,128)}, u32[]{:S(2)}) copy-start(f32[2,120,512]{2,1,0:T(8,128)} %param.5) | copy-start | bytes 1474564
Sparse Core Ops, SparseCore 0:
  20.9 204.2 all-gather.2
where the time goes:
time: 355 us
  waiting for transfers between devices  199 us (56%)
  local copies, waits for them, and re-layouts  63.7 us (18%)
  other arithmetic  47.8 us (13%)
  matrix products  18.9 us (5%)
  between operations  14.2 us (4%)
  blocking collectives  6 us (2%)
  starting transfers between devices  4.92 us (1%)
    all_gather x1, waiting for transfers between devices, shards(): lax.all_gather(local_eof, 'tm', axis=1, tiled=True)  178 us
    ppermute x1, waiting for transfers between devices, padded_2(): lax.ppermute(lax.slice_in_dim(block, block.shape[dim] - width, None, axis...  20.9 us
    slice x2, local copies, waits for them, and re-layouts, curl_div(): jnp.roll(inner_east, 1, axis=2)  19.9 us
    gather x2, local copies, waits for them, and re-layouts, lagged_rc(): values_lag = jnp.where(inside[None], series[:, safe_index], 0.0)  18.8 us
    dot_general x1, matrix products, shards(): jnp.einsum('tc,xcn->txn', own_rc, lax.all_gather(local_eof, 'tm', axis=1,...  18.5 us
    mul x1, other arithmetic, shards(): return (vorticity * ocean_mask[None], divergence * ocean_mask[None])  18.3 us
    reshape x1, local copies, waits for them, and re-layouts, shards(): local_eof = spatial_eof.reshape(2, chan_share, cell_count)  13.6 us
    convert_element_type x1, other arithmetic, shards(): padded[:, 0].astype(jnp.float32)  11.3 us
  transfers between devices with their start and end apart: 3, of which 2 were waited for; matrix products, arithmetic and copies ran while one was open for 6% of the time, Pallas kernels for 0%

commit v1 on v0

v1 whole, which is shorter than its diff:
```python
import functools
import math

import jax
import jax.numpy as jnp
from jax import lax
from jax.experimental import pallas as pl
from jax.experimental.pallas import tpu as pltpu
from jax.sharding import PartitionSpec as P

MESH = pl.DeviceIdType.MESH
F32 = jnp.float32
BF16 = jnp.bfloat16


def iota(shape, axis):
    return lax.broadcasted_iota(jnp.int32, shape, axis)


def kernel(
    dims,
    pcs_ref,
    st_ref,
    eof_ref,
    mask_ref,
    coef_ref,
    vort_ref,
    div_ref,
    pcs_slots,
    st_buf,
    eof_buf,
    mix,
    send_buf,
    recv_buf,
    vel,
    halo_send,
    halo_recv,
    out_buf,
    st_sem,
    pcs_ssem,
    pcs_rsem,
    eof_lsem,
    eof_ssem,
    eof_rsem,
    part_ssem,
    part_rsem,
    halo_ssem,
    halo_rsem,
    out_sem,
):
    n_tm, n_tile, days, lat, width, chunks, lags, chan = dims
    rows = days * lat
    depth = chan * lat
    me = lax.axis_index("tm")
    tile = lax.axis_index("tile")
    partner = me + 1 - 2 * lax.rem(me, 2)
    cross = lax.rem(me + n_tm // 2, n_tm)
    has_low = tile > 0
    has_high = tile < n_tile - 1

    st_copy = pltpu.make_async_copy(st_ref, st_buf.at[:, pl.ds(0, lags)], st_sem)
    st_copy.start()

    def eof_local(n):
        src = eof_ref.at[:, :, pl.ds(pl.multiple_of(n * width, width), width)]
        return pltpu.make_async_copy(src, eof_buf.at[n, :, pl.ds(0, depth)], eof_lsem.at[n])

    def eof_remote(n):
        src = eof_ref.at[:, :, pl.ds(pl.multiple_of(n * width, width), width)]
        return pltpu.make_async_remote_copy(
            src_ref=src,
            dst_ref=eof_buf.at[n, :, pl.ds(depth, depth)],
            send_sem=eof_ssem.at[n],
            recv_sem=eof_rsem.at[n],
            device_id=(partner, tile),
            device_id_type=MESH,
        )

    def part_copy(n):
        return pltpu.make_async_remote_copy(
            src_ref=send_buf.at[n],
            dst_ref=recv_buf.at[n],
            send_sem=part_ssem.at[n],
            recv_sem=part_rsem.at[n],
            device_id=(cross, tile),
            device_id_type=MESH,
        )

    def halo_down(n):
        return pltpu.make_async_remote_copy(
            src_ref=halo_send.at[n, :, pl.ds(0, days)],
            dst_ref=halo_recv.at[n, :, pl.ds(days, days)],
            send_sem=halo_ssem.at[0, n],
            recv_sem=halo_rsem.at[0, n],
            device_id=(me, tile - 1),
            device_id_type=MESH,
        )

    def halo_up(n):
        return pltpu.make_async_remote_copy(
            src_ref=halo_send.at[n, :, pl.ds(days, days)],
            dst_ref=halo_recv.at[n, :, pl.ds(0, days)],
            send_sem=halo_ssem.at[1, n],
            recv_sem=halo_rsem.at[1, n],
            device_id=(me, tile + 1),
            device_id_type=MESH,
        )

    def out_copies(n):
        cols = pl.ds(pl.multiple_of(n * width, width), width)
        return [
            pltpu.make_async_copy(out_buf.at[n, q], ref.at[:, cols], out_sem.at[q, n])
            for q, ref in enumerate((vort_ref, div_ref))
        ]

    lax.fori_loop(0, chunks, lambda n, c: (eof_local(n).start(), c)[1], 0)

    barrier = pltpu.get_barrier_semaphore()
    for step in range(1, n_tm):
        pl.semaphore_signal(
            barrier, inc=1, device_id=(lax.rem(me + step, n_tm), tile), device_id_type=MESH
        )

    @pl.when(has_low)
    def _():
        pl.semaphore_signal(barrier, inc=1, device_id=(me, tile - 1), device_id_type=MESH)

    @pl.when(has_high)
    def _():
        pl.semaphore_signal(barrier, inc=1, device_id=(me, tile + 1), device_id_type=MESH)

    neighbours = has_low.astype(jnp.int32) + has_high.astype(jnp.int32)
    pl.semaphore_wait(barrier, n_tm - 1 + neighbours)

    pcs_copies = []
    for step in range(1, n_tm):
        copy = pltpu.make_async_remote_copy(
            src_ref=pcs_ref,
            dst_ref=pcs_slots.at[step - 1],
            send_sem=pcs_ssem.at[step - 1],
            recv_sem=pcs_rsem.at[step - 1],
            device_id=(lax.rem(me + step, n_tm), tile),
            device_id_type=MESH,
        )
        copy.start()
        pcs_copies.append(copy)
    lax.fori_loop(0, chunks, lambda n, c: (eof_remote(n).start(), c)[1], 0)

    lag_pad = st_buf.shape[1]
    if lag_pad > lags:
        st_buf[:, lags:] = jnp.zeros((st_buf.shape[0], lag_pad - lags, st_buf.shape[2]), F32)

    @pl.when(jnp.logical_not(has_low))
    def _():
        halo_recv[:, :, pl.ds(0, days)] = jnp.zeros((chunks, 2, days, width), BF16)

    @pl.when(jnp.logical_not(has_high))
    def _():
        halo_recv[:, :, pl.ds(days, days)] = jnp.zeros((chunks, 2, days, width), BF16)

    st_copy.wait()
    backward = pcs_ref[...]
    for copy in pcs_copies:
        copy.wait()
    for step in range(1, n_tm):
        backward = backward + pcs_slots[step - 1]
    total_days = backward.shape[1]

    repeat_rows = (
        (iota((rows, days), 0) >= iota((rows, days), 1) * lat)
        & (iota((rows, days), 0) < iota((rows, days), 1) * lat + lat)
    ).astype(BF16)
    piece = 2 * 128
    for slot, target in enumerate((cross, me)):
        first = target * days
        day = first + iota((days, lag_pad), 0)
        lag = iota((days, lag_pad), 1)
        inside = (lag <= day) & (lag < lags)
        lagged = []
        for k in range(st_buf.shape[0]):
            wide = jnp.broadcast_to(backward[k : k + 1], (days, total_days))
            wide = pltpu.roll(wide, first + 1, 1)
            at = iota((days, total_days), 0)
            bit = 1
            while bit < days:
                wide = jnp.where((at & bit) != 0, pltpu.roll(wide, bit, 1), wide)
                bit *= 2
            lagged.append(jnp.where(inside, wide[:, :lag_pad], 0.0))
        window = jnp.minimum(first + iota((days, chan), 0) + 1, lags).astype(F32)
        for part, owner in enumerate((me, partner)):
            cols = pl.ds(pl.multiple_of(owner * chan, chan), chan)
            sums = jnp.zeros((days, chan), F32)
            for k in range(st_buf.shape[0]):
                sums = sums + jnp.dot(
                    lagged[k],
                    st_buf[k, :, cols],
                    precision=lax.Precision.HIGHEST,
                    preferred_element_type=F32,
                )
            comp = (sums / window).astype(BF16)
            tall = jnp.dot(repeat_rows, comp, preferred_element_type=F32).astype(BF16)
            for start in range(0, depth, piece):
                c_at = iota((chan, piece), 0) * lat
                col_at = iota((chan, piece), 1) + start
                expand = ((col_at >= c_at) & (col_at < c_at + lat)).astype(BF16)
                spread = jnp.dot(tall, expand, preferred_element_type=F32)
                same = (iota((rows, piece), 0) & (lat - 1)) == (iota((rows, piece), 1) & (lat - 1))
                mix[slot, :, part * depth + start : part * depth + start + piece] = jnp.where(
                    same, spread, 0.0
                ).astype(BF16)

    def send_part(n, carry):
        eof_local(n).wait()
        eof_remote(n).wait_recv()
        for x in range(2):
            send_buf[n, x] = jnp.dot(
                mix[0], eof_buf[n, x], preferred_element_type=F32
            ).astype(BF16)
        part_copy(n).start()
        return carry

    lax.fori_loop(0, chunks, send_part, 0)

    edge = iota((2 * days, rows), 0)
    row = iota((2 * days, rows), 1)
    pick = ((edge < days) & (row == edge * lat)) | (
        (edge >= days) & (row == (edge - days) * lat + lat - 1)
    )
    edge_t = iota((rows, 2 * days), 1)
    row_t = iota((rows, 2 * days), 0)
    place = ((edge_t < days) & (row_t == edge_t * lat)) | (
        (edge_t >= days) & (row_t == (edge_t - days) * lat + lat - 1)
    )
    pick = pick.astype(BF16)
    place = place.astype(BF16)

    def make_velocity(n):
        own = [jnp.dot(mix[1], eof_buf[n, x], preferred_element_type=F32) for x in range(2)]
        part_copy(n).wait_recv()
        ocean = mask_ref[:, pl.ds(pl.multiple_of(n * width, width), width)].astype(F32)
        for x in range(2):
            total = (own[x] + recv_buf[n, x].astype(F32)).reshape(days, lat, width)
            vel[n, x] = (total * ocean[None]).reshape(rows, width).astype(BF16)
        for x in range(2):
            halo_send[n, x] = jnp.dot(pick, vel[n, x], preferred_element_type=F32).astype(BF16)

        @pl.when(has_low)
        def _():
            halo_down(n).start()

        @pl.when(has_high)
        def _():
            halo_up(n).start()

    def stencil(n):
        before = lax.rem(n + chunks - 1, chunks)
        after = lax.rem(n + 1, chunks)

        @pl.when(has_low)
        def _():
            halo_up(n).wait_recv()

        @pl.when(has_high)
        def _():
            halo_down(n).wait_recv()

        shape = (days, lat, width)
        lane = iota((lat, width), 1)[None]
        line = iota((lat, width), 0)[None]
        cosine = coef_ref[0:lat][None]
        outer = coef_ref[lat : 2 * lat][None]
        ocean = mask_ref[:, pl.ds(pl.multiple_of(n * width, width), width)].astype(F32)
        scale = (ocean * coef_ref[2 * lat : 3 * lat])[None]
        zonal = []
        meridional = []
        for x in range(2):
            here = vel[n, x].astype(F32).reshape(rows, width)
            west = vel[before, x].astype(F32)
            east = vel[after, x].astype(F32)
            up = jnp.where(
                lane == width - 1,
                pltpu.roll(east, width - 1, 1).reshape(shape),
                pltpu.roll(here, width - 1, 1).reshape(shape),
            )
            down = jnp.where(
                lane == 0,
                pltpu.roll(west, 1, 1).reshape(shape),
                pltpu.roll(here, 1, 1).reshape(shape),
            )
            zonal.append(up - down)
            edges = jnp.dot(place, halo_recv[n, x], preferred_element_type=F32).reshape(shape) * outer
            weighted = here.reshape(shape) * cosine
            north = jnp.where(line == lat - 1, edges, pltpu.roll(weighted, lat - 1, 1))
            south = jnp.where(line == 0, edges, pltpu.roll(weighted, 1, 1))
            meridional.append(north - south)
        out_buf[n, 0] = ((zonal[1] - meridional[0]) * scale).reshape(rows, width)
        out_buf[n, 1] = ((zonal[0] + meridional[1]) * scale).reshape(rows, width)
        for copy in out_copies(n):
            copy.start()

    def finish(step, carry):
        @pl.when(step < chunks)
        def _():
            make_velocity(step)

        @pl.when(step >= 2)
        def _():
            stencil(lax.rem(step - 1, chunks))

        return carry

    lax.fori_loop(0, chunks + 2, finish, 0)

    def drain(n, carry):
        eof_remote(n).wait_send()
        part_copy(n).wait_send()

        @pl.when(has_low)
        def _():
            halo_down(n).wait_send()

        @pl.when(has_high)
        def _():
            halo_up(n).wait_send()

        for copy in out_copies(n):
            copy.wait()
        return carry

    lax.fori_loop(0, chunks, drain, 0)


def shards(pcs, st_eof, spatial_eof, land_sea):
    n_tm = lax.axis_size("tm")
    n_tile = lax.axis_size("tile")
    pairs, days = pcs.shape
    lags = st_eof.shape[1]
    lat, lon = land_sea.shape
    chan = spatial_eof.shape[1]
    rows = days * lat
    depth = chan * lat
    width = 256
    chunks = lon // width
    lag_pad = -(-lags // 128) * 128
    total_days = days * n_tm

    start = total_days - days - lax.axis_index("tm") * days
    placed = lax.dynamic_update_slice(
        jnp.zeros((8, total_days), F32), pcs[:, ::-1], (jnp.int32(0), start)
    )
    total_lat = lat * n_tile
    base = (lax.axis_index("tile") * lat).astype(F32)

    def cos_at(rows_at):
        return jnp.cos((-70.0 + 140.0 * (rows_at + 0.5) / total_lat) * (math.pi / 180.0))

    inner = cos_at(base + jnp.arange(lat, dtype=F32))
    place = jnp.arange(lat, dtype=F32)
    outer = jnp.where(
        place == 0, cos_at(base - 1.0), jnp.where(place == lat - 1, cos_at(base + lat), 0.0)
    )
    coef = jnp.broadcast_to(
        jnp.concatenate([inner, outer, 1.0 / (2.0 * inner)])[:, None], (3 * lat, width)
    )
    dims = (n_tm, n_tile, days, lat, width, chunks, lags, chan)
    dma = pltpu.SemaphoreType.DMA
    vmem = pl.BlockSpec(memory_space=pltpu.VMEM)
    hbm = pl.BlockSpec(memory_space=pl.ANY)
    vorticity, divergence = pl.pallas_call(
        functools.partial(kernel, dims),
        out_shape=[jax.ShapeDtypeStruct((rows, lon), F32)] * 2,
        in_specs=[vmem, hbm, hbm, vmem, vmem],
        out_specs=[hbm, hbm],
        scratch_shapes=[
            pltpu.VMEM((n_tm - 1, 8, total_days), F32),
            pltpu.VMEM((pairs, lag_pad, st_eof.shape[2]), F32),
            pltpu.VMEM((chunks, 2, 2 * depth, width), BF16),
            pltpu.VMEM((2, rows, 2 * depth), BF16),
            pltpu.VMEM((chunks, 2, rows, width), BF16),
            pltpu.VMEM((chunks, 2, rows, width), BF16),
            pltpu.VMEM((chunks, 2, rows, width), BF16),
            pltpu.VMEM((chunks, 2, 2 * days, width), BF16),
            pltpu.VMEM((chunks, 2, 2 * days, width), BF16),
            pltpu.VMEM((chunks, 2, rows, width), F32),
            dma,
            dma((n_tm - 1,)),
            dma((n_tm - 1,)),
            dma((chunks,)),
            dma((chunks,)),
            dma((chunks,)),
            dma((chunks,)),
            dma((chunks,)),
            dma((2, chunks)),
            dma((2, chunks)),
            dma((2, chunks)),
        ],
        compiler_params=pltpu.CompilerParams(
            collective_id=0, has_side_effects=True, vmem_limit_bytes=62 * 1024 * 1024
        ),
        name="reconstruct",
    )(placed, st_eof, spatial_eof.reshape(2, depth, lon), land_sea, coef)
    return vorticity.reshape(days, lat, lon), divergence.reshape(days, lat, lon)


def solution(mesh):
    return jax.shard_map(
        shards,
        mesh=mesh,
        in_specs=(P(None, "tm"), P(), P(None, "tm", "tile", None), P("tile", None)),
        out_specs=(P("tm", "tile", None), P("tm", "tile", None)),
        check_vma=False,
    )
```

time: 355 us -> 123 us (0.35)
  waiting for transfers between devices: 199 us -> 0 us
  Pallas kernels: 0 us -> 113 us
  local copies, waits for them, and re-layouts: 63.7 us -> 8.73 us
  other arithmetic: 47.8 us -> 0.14 us
  matrix products: 18.9 us -> 0 us
  between operations: 14.2 us -> 0.83 us
  blocking collectives: 6 us -> 0 us
  starting transfers between devices: 4.92 us -> 0 us
    all_gather x1 -> x0, waiting for transfers between devices: 178 us -> none  [shards(): lax.all_gather(local_eof, 'tm', axis=1, tiled=True)]
    pallas_call x0 -> x1, Pallas kernels: none -> 113 us  [shards(): pl.pallas_call(functools.partial(kernel, dims), out_shape=[jax.ShapeDtype...]
    mul x3 -> x0, other arithmetic: 27.7 us -> none  [the longest x1 18.3 us: shards(): return (vorticity * ocean_mask[None], divergence * ocean_mask[None])]
    slice x3 -> x0, local copies, waits for them, and re-layouts: 21.4 us -> none  [the longest x2 19.9 us: curl_div(): jnp.roll(inner_east, 1, axis=2)]
    ppermute x2 -> x0, waiting for transfers between devices: 20.9 us -> none  [the longest x1 20.9 us: padded_2(): lax.ppermute(lax.slice_in_dim(block, block.shape[dim] - width, None, axis...]
    dot_general x2 -> x0, matrix products: 18.9 us -> none  [the longest x1 18.5 us: shards(): jnp.einsum('tc,xcn->txn', own_rc, lax.all_gather(local_eof, 'tm', axis=1,...]
    gather x2 -> x0, local copies, waits for them, and re-layouts: 18.8 us -> none  [lagged_rc(): values_lag = jnp.where(inside[None], series[:, safe_index], 0.0)]
    reshape x1 -> x0, local copies, waits for them, and re-layouts: 13.6 us -> none  [shards(): local_eof = spatial_eof.reshape(2, chan_share, cell_count)]
  transfers between devices with their start and end apart: 3 -> 0, of which waited for: 2 -> 0; matrix products, arithmetic and copies ran while one was open for 6% -> 0% of each run, Pallas kernels for 0% -> 0%
where the time goes in v1:
time: 123 us; the launch traced here: 122 us
  Pallas kernels  113 us (92%)
  local copies, waits for them, and re-layouts  8.73 us (7%)
    pallas_call x1, Pallas kernels, shards(): pl.pallas_call(functools.partial(kernel, dims), out_shape=[jax.ShapeDtype...  113 us
    unnamed x6, local copies, waits for them, and re-layouts  6.87 us

profile of v1, /device:TPU:0, one launch (start us, length us, event | category | flops | bytes accessed | tf_op | source)
XLA Modules:
  0.0 122.4 jit_solution(5209277308827792681)
XLA Ops:
  0.8 0.1 multiply_divide_fusion
  0.9 0.1 pad_maximum_fusion
  0.9 0.8 rev.3
  1.7 0.4 dynamic_update_slice.3.pcs_ref
  2.1 0.0 copy-start.1
  2.1 0.7 broadcast_in_dim.22.coef_ref
  2.8 0.0 copy-done.1
  2.8 112.7 %reconstruct.1 = (f32[512,2048]{1,0:T(8,128)}, f32[512,2048]{1,0:T(8,128)}) custom-call(f32[8,256]{1,0:T(8,128)} %copy-done.1, f32[2,120,512]{2,1,0:T(8,128)} %st_ref.1, bf16[2,1024,2048]{2,1,0:T(8,128)(2,1)} %bitcast.3, s32[8,2048]{1,0:T(8,128)} %mask_ref.1, f32[24,256]{1,0:T(8,128)} %broadcast_in_dim.22.coef_ref), custom_call_target="tpu_custom_call" | custom-call | tf_op jit(solution)/shard_map/reconstruct/pallas_call | solution.py:369
  115.6 0.0 copy-start
  115.6 4.8 %copy.9 = f32[64,8,2048]{2,1,0:T(8,128)} copy(f32[64,8,2048]{2,1,0:T(8,128)} %bitcast.5) | data formatting | bytes 8388608
  120.4 0.0 copy-done
  120.4 2.0 %copy.10 = f32[64,8,2048]{2,1,0:T(8,128)} copy(f32[64,8,2048]{2,1,0:T(8,128)S(1)} %bitcast.4) | data formatting | bytes 8388608
  (2 shorter events, 0.0 us)
Async XLA Ops:
  2.1 0.7 copy-start.1
  115.6 4.9 %copy-start = (f32[512,2048]{1,0:T(8,128)S(1)}, f32[512,2048]{1,0:T(8,128)}, u32[]{:S(2)}) copy-start(f32[512,2048]{1,0:T(8,128)} %get-tuple-element.5) | copy-start | bytes 12582916

commit v2 on v1

--- a/solution.py
+++ b/solution.py
@@ -23,7 +23,6 @@
     st_ref,
     eof_ref,
     mask_ref,
-    coef_ref,
     vort_ref,
     div_ref,
     pcs_slots,
@@ -36,6 +35,7 @@
     halo_send,
     halo_recv,
     out_buf,
+    coef_ref,
     st_sem,
     pcs_ssem,
     pcs_rsem,
@@ -76,12 +76,12 @@
             device_id_type=MESH,
         )
 
-    def part_copy(n):
+    def part_copy(n, x):
         return pltpu.make_async_remote_copy(
-            src_ref=send_buf.at[n],
-            dst_ref=recv_buf.at[n],
-            send_sem=part_ssem.at[n],
-            recv_sem=part_rsem.at[n],
+            src_ref=send_buf.at[n, x],
+            dst_ref=recv_buf.at[n, x],
+            send_sem=part_ssem.at[x, n],
+            recv_sem=part_rsem.at[x, n],
             device_id=(cross, tile),
             device_id_type=MESH,
         )
@@ -159,19 +159,26 @@
         halo_recv[:, :, pl.ds(days, days)] = jnp.zeros((chunks, 2, days, width), BF16)
 
     st_copy.wait()
-    backward = pcs_ref[...]
     for copy in pcs_copies:
         copy.wait()
-    for step in range(1, n_tm):
-        backward = backward + pcs_slots[step - 1]
-    total_days = backward.shape[1]
+    total_days = days * n_tm
+    backward = jnp.zeros((st_buf.shape[0], total_days), F32)
+    for step in range(n_tm):
+        owner = lax.rem(me + n_tm - step, n_tm)
+        days_of = pcs_ref[...] if step == 0 else pcs_slots[step - 1]
+        at_day = iota((days, total_days), 0) + iota((days, total_days), 1)
+        spot = (at_day == total_days - 1 - owner * days).astype(F32)
+        backward = backward + jnp.dot(
+            days_of, spot, precision=lax.Precision.HIGHEST, preferred_element_type=F32
+        )
 
     repeat_rows = (
         (iota((rows, days), 0) >= iota((rows, days), 1) * lat)
         & (iota((rows, days), 0) < iota((rows, days), 1) * lat + lat)
     ).astype(BF16)
     piece = 2 * 128
-    for slot, target in enumerate((cross, me)):
+
+    def build_mix(slot, target):
         first = target * days
         day = first + iota((days, lag_pad), 0)
         lag = iota((days, lag_pad), 1)
@@ -209,6 +216,8 @@
                     same, spread, 0.0
                 ).astype(BF16)
 
+    build_mix(0, cross)
+
     def send_part(n, carry):
         eof_local(n).wait()
         eof_remote(n).wait_recv()
@@ -216,10 +225,27 @@
             send_buf[n, x] = jnp.dot(
                 mix[0], eof_buf[n, x], preferred_element_type=F32
             ).astype(BF16)
-        part_copy(n).start()
+            part_copy(n, x).start()
         return carry
 
     lax.fori_loop(0, chunks, send_part, 0)
+    build_mix(1, me)
+
+    line_at = tile * lat + iota((lat, width), 0)
+    at_line = iota((lat, width), 0)
+
+    def cos_at(lines):
+        degrees = -70.0 + 140.0 * (lines.astype(F32) + 0.5) / (lat * n_tile)
+        return jnp.cos(degrees * (math.pi / 180.0))
+
+    inner = cos_at(line_at)
+    coef_ref[0:lat] = inner
+    coef_ref[lat : 2 * lat] = jnp.where(
+        at_line == 0,
+        cos_at(line_at - 1),
+        jnp.where(at_line == lat - 1, cos_at(line_at + 1), 0.0),
+    )
+    coef_ref[2 * lat : 3 * lat] = 1.0 / (2.0 * inner)
 
     edge = iota((2 * days, rows), 0)
     row = iota((2 * days, rows), 1)
@@ -236,12 +262,11 @@
 
     def make_velocity(n):
         own = [jnp.dot(mix[1], eof_buf[n, x], preferred_element_type=F32) for x in range(2)]
-        part_copy(n).wait_recv()
         ocean = mask_ref[:, pl.ds(pl.multiple_of(n * width, width), width)].astype(F32)
         for x in range(2):
+            part_copy(n, x).wait_recv()
             total = (own[x] + recv_buf[n, x].astype(F32)).reshape(days, lat, width)
             vel[n, x] = (total * ocean[None]).reshape(rows, width).astype(BF16)
-        for x in range(2):
             halo_send[n, x] = jnp.dot(pick, vel[n, x], preferred_element_type=F32).astype(BF16)
 
         @pl.when(has_low)
@@ -305,7 +330,7 @@
 
         @pl.when(step >= 2)
         def _():
-            stencil(lax.rem(step - 1, chunks))
+            stencil(jnp.where(step >= chunks, (step - chunks) * (chunks - 1), step - 1))
 
         return carry
 
@@ -313,7 +338,8 @@
 
     def drain(n, carry):
         eof_remote(n).wait_send()
-        part_copy(n).wait_send()
+        for x in range(2):
+            part_copy(n, x).wait_send()
 
         @pl.when(has_low)
         def _():
@@ -342,26 +368,6 @@
     width = 256
     chunks = lon // width
     lag_pad = -(-lags // 128) * 128
-    total_days = days * n_tm
-
-    start = total_days - days - lax.axis_index("tm") * days
-    placed = lax.dynamic_update_slice(
-        jnp.zeros((8, total_days), F32), pcs[:, ::-1], (jnp.int32(0), start)
-    )
-    total_lat = lat * n_tile
-    base = (lax.axis_index("tile") * lat).astype(F32)
-
-    def cos_at(rows_at):
-        return jnp.cos((-70.0 + 140.0 * (rows_at + 0.5) / total_lat) * (math.pi / 180.0))
-
-    inner = cos_at(base + jnp.arange(lat, dtype=F32))
-    place = jnp.arange(lat, dtype=F32)
-    outer = jnp.where(
-        place == 0, cos_at(base - 1.0), jnp.where(place == lat - 1, cos_at(base + lat), 0.0)
-    )
-    coef = jnp.broadcast_to(
-        jnp.concatenate([inner, outer, 1.0 / (2.0 * inner)])[:, None], (3 * lat, width)
-    )
     dims = (n_tm, n_tile, days, lat, width, chunks, lags, chan)
     dma = pltpu.SemaphoreType.DMA
     vmem = pl.BlockSpec(memory_space=pltpu.VMEM)
@@ -369,10 +375,10 @@
     vorticity, divergence = pl.pallas_call(
         functools.partial(kernel, dims),
         out_shape=[jax.ShapeDtypeStruct((rows, lon), F32)] * 2,
-        in_specs=[vmem, hbm, hbm, vmem, vmem],
+        in_specs=[vmem, hbm, hbm, vmem],
         out_specs=[hbm, hbm],
         scratch_shapes=[
-            pltpu.VMEM((n_tm - 1, 8, total_days), F32),
+            pltpu.VMEM((n_tm - 1, pairs, days), F32),
             pltpu.VMEM((pairs, lag_pad, st_eof.shape[2]), F32),
             pltpu.VMEM((chunks, 2, 2 * depth, width), BF16),
             pltpu.VMEM((2, rows, 2 * depth), BF16),
@@ -382,14 +388,15 @@
             pltpu.VMEM((chunks, 2, 2 * days, width), BF16),
             pltpu.VMEM((chunks, 2, 2 * days, width), BF16),
             pltpu.VMEM((chunks, 2, rows, width), F32),
+            pltpu.VMEM((3 * lat, width), F32),
             dma,
             dma((n_tm - 1,)),
             dma((n_tm - 1,)),
             dma((chunks,)),
             dma((chunks,)),
             dma((chunks,)),
-            dma((chunks,)),
-            dma((chunks,)),
+            dma((2, chunks)),
+            dma((2, chunks)),
             dma((2, chunks)),
             dma((2, chunks)),
             dma((2, chunks)),
@@ -398,7 +405,7 @@
             collective_id=0, has_side_effects=True, vmem_limit_bytes=62 * 1024 * 1024
         ),
         name="reconstruct",
-    )(placed, st_eof, spatial_eof.reshape(2, depth, lon), land_sea, coef)
+    )(pcs, st_eof, spatial_eof.reshape(2, depth, lon), land_sea)
     return vorticity.reshape(days, lat, lon), divergence.reshape(days, lat, lon)
 
 

time: 123 us -> 118 us (0.959)
  Pallas kernels: 113 us -> 110 us
  local copies, waits for them, and re-layouts: 8.73 us -> 6.87 us
    pallas_call x1, Pallas kernels: 113 us -> 110 us  [shards(): pl.pallas_call(functools.partial(kernel, dims), out_shape=[jax.ShapeDtype...]
    unnamed x6 -> x4, local copies, waits for them, and re-layouts: 6.87 us -> 6.87 us
where the time goes in v2:
time: 118 us
  Pallas kernels  110 us (93%)
  local copies, waits for them, and re-layouts  6.87 us (6%)
    pallas_call x1, Pallas kernels, shards(): pl.pallas_call(functools.partial(kernel, dims), out_shape=[jax.ShapeDtype...  110 us
    unnamed x4, local copies, waits for them, and re-layouts  6.87 us

profile of v2, /device:TPU:0, one launch (start us, length us, event | category | flops | bytes accessed | tf_op | source)
XLA Modules:
  0.0 117.9 jit_solution(3652660860450133067)
XLA Ops:
  0.6 110.3 %reconstruct.1 = (f32[512,2048]{1,0:T(8,128)}, f32[512,2048]{1,0:T(8,128)}) custom-call(f32[2,64]{1,0:T(2,128)} %pcs_ref.1, f32[2,120,512]{2,1,0:T(8,128)} %st_ref.1, bf16[2,1024,2048]{2,1,0:T(8,128)(2,1)} %bitcast.3, s32[8,2048]{1,0:T(8,128)} %mask_ref.1), custom_call_target="tpu_custom_call" | custom-call | tf_op jit(solution)/shard_map/reconstruct/pallas_call | solution.py:375
  111.0 0.0 copy-start
  111.0 4.8 %copy.8 = f32[64,8,2048]{2,1,0:T(8,128)} copy(f32[64,8,2048]{2,1,0:T(8,128)} %bitcast.5) | data formatting | bytes 8388608
  115.8 0.0 copy-done
  115.8 2.0 %copy.9 = f32[64,8,2048]{2,1,0:T(8,128)} copy(f32[64,8,2048]{2,1,0:T(8,128)S(1)} %bitcast.4) | data formatting | bytes 8388608
Async XLA Ops:
  111.0 4.9 %copy-start = (f32[512,2048]{1,0:T(8,128)S(1)}, f32[512,2048]{1,0:T(8,128)}, u32[]{:S(2)}) copy-start(f32[512,2048]{1,0:T(8,128)} %get-tuple-element.5) | copy-start | bytes 12582916

commit v3 on v2

--- a/solution.py
+++ b/solution.py
@@ -36,6 +36,7 @@
     halo_recv,
     out_buf,
     coef_ref,
+    edge_buf,
     st_sem,
     pcs_ssem,
     pcs_rsem,
@@ -289,37 +290,46 @@
         def _():
             halo_down(n).wait_recv()
 
-        shape = (days, lat, width)
+        for x in range(2):
+            edge_buf[x] = jnp.dot(place, halo_recv[n, x], preferred_element_type=F32)
+        group = 4 * lat
+        shape = (4, lat, width)
         lane = iota((lat, width), 1)[None]
         line = iota((lat, width), 0)[None]
         cosine = coef_ref[0:lat][None]
         outer = coef_ref[lat : 2 * lat][None]
         ocean = mask_ref[:, pl.ds(pl.multiple_of(n * width, width), width)].astype(F32)
         scale = (ocean * coef_ref[2 * lat : 3 * lat])[None]
-        zonal = []
-        meridional = []
-        for x in range(2):
-            here = vel[n, x].astype(F32).reshape(rows, width)
-            west = vel[before, x].astype(F32)
-            east = vel[after, x].astype(F32)
-            up = jnp.where(
-                lane == width - 1,
-                pltpu.roll(east, width - 1, 1).reshape(shape),
-                pltpu.roll(here, width - 1, 1).reshape(shape),
-            )
-            down = jnp.where(
-                lane == 0,
-                pltpu.roll(west, 1, 1).reshape(shape),
-                pltpu.roll(here, 1, 1).reshape(shape),
-            )
-            zonal.append(up - down)
-            edges = jnp.dot(place, halo_recv[n, x], preferred_element_type=F32).reshape(shape) * outer
-            weighted = here.reshape(shape) * cosine
-            north = jnp.where(line == lat - 1, edges, pltpu.roll(weighted, lat - 1, 1))
-            south = jnp.where(line == 0, edges, pltpu.roll(weighted, 1, 1))
-            meridional.append(north - south)
-        out_buf[n, 0] = ((zonal[1] - meridional[0]) * scale).reshape(rows, width)
-        out_buf[n, 1] = ((zonal[0] + meridional[1]) * scale).reshape(rows, width)
+
+        def days_of(b, carry):
+            at = pl.ds(pl.multiple_of(b * group, group), group)
+            zonal = []
+            meridional = []
+            for x in range(2):
+                here = vel[n, x, at].astype(F32)
+                west = vel[before, x, at, width - 128 :].astype(F32)
+                east = vel[after, x, at, :128].astype(F32)
+                west = jnp.concatenate([pltpu.roll(west, 1, 1), here[:, 128:]], axis=1)
+                east = jnp.concatenate([here[:, :-128], pltpu.roll(east, 127, 1)], axis=1)
+                up = jnp.where(
+                    lane == width - 1,
+                    east.reshape(shape),
+                    pltpu.roll(here, width - 1, 1).reshape(shape),
+                )
+                down = jnp.where(
+                    lane == 0, west.reshape(shape), pltpu.roll(here, 1, 1).reshape(shape)
+                )
+                zonal.append(up - down)
+                edges = edge_buf[x, at].reshape(shape) * outer
+                weighted = here.reshape(shape) * cosine
+                north = jnp.where(line == lat - 1, edges, pltpu.roll(weighted, lat - 1, 1))
+                south = jnp.where(line == 0, edges, pltpu.roll(weighted, 1, 1))
+                meridional.append(north - south)
+            out_buf[n, 0, at] = ((zonal[1] - meridional[0]) * scale).reshape(group, width)
+            out_buf[n, 1, at] = ((zonal[0] + meridional[1]) * scale).reshape(group, width)
+            return carry
+
+        lax.fori_loop(0, rows // group, days_of, 0)
         for copy in out_copies(n):
             copy.start()
 
@@ -389,6 +399,7 @@
             pltpu.VMEM((chunks, 2, 2 * days, width), BF16),
             pltpu.VMEM((chunks, 2, rows, width), F32),
             pltpu.VMEM((3 * lat, width), F32),
+            pltpu.VMEM((2, rows, width), F32),
             dma,
             dma((n_tm - 1,)),
             dma((n_tm - 1,)),

time: 118 us -> 119 us (level)
  no operation moved by 1% of the time
where the time goes in v3:
time: 119 us
  Pallas kernels  111 us (93%)
  local copies, waits for them, and re-layouts  6.87 us (6%)
    pallas_call x1, Pallas kernels, shards(): pl.pallas_call(functools.partial(kernel, dims), out_shape=[jax.ShapeDtype...  111 us
    unnamed x4, local copies, waits for them, and re-layouts  6.87 us

profile of v3, /device:TPU:0, one launch (start us, length us, event | category | flops | bytes accessed | tf_op | source)
XLA Modules:
  0.0 118.7 jit_solution(11038477308984558542)
XLA Ops:
  0.6 111.2 %reconstruct.1 = (f32[512,2048]{1,0:T(8,128)}, f32[512,2048]{1,0:T(8,128)}) custom-call(f32[2,64]{1,0:T(2,128)} %pcs_ref.1, f32[2,120,512]{2,1,0:T(8,128)} %st_ref.1, bf16[2,1024,2048]{2,1,0:T(8,128)(2,1)} %bitcast.3, s32[8,2048]{1,0:T(8,128)} %mask_ref.1), custom_call_target="tpu_custom_call" | custom-call | tf_op jit(solution)/shard_map/reconstruct/pallas_call | solution.py:385
  111.8 0.0 copy-start
  111.9 4.8 %copy.8 = f32[64,8,2048]{2,1,0:T(8,128)} copy(f32[64,8,2048]{2,1,0:T(8,128)} %bitcast.5) | data formatting | bytes 8388608
  116.7 0.0 copy-done
  116.7 2.0 %copy.9 = f32[64,8,2048]{2,1,0:T(8,128)} copy(f32[64,8,2048]{2,1,0:T(8,128)S(1)} %bitcast.4) | data formatting | bytes 8388608
Async XLA Ops:
  111.8 4.9 %copy-start = (f32[512,2048]{1,0:T(8,128)S(1)}, f32[512,2048]{1,0:T(8,128)}, u32[]{:S(2)}) copy-start(f32[512,2048]{1,0:T(8,128)} %get-tuple-element.5) | copy-start | bytes 12582916

commit v4 on v2

--- a/solution.py
+++ b/solution.py
@@ -61,17 +61,17 @@
     st_copy = pltpu.make_async_copy(st_ref, st_buf.at[:, pl.ds(0, lags)], st_sem)
     st_copy.start()
 
-    def eof_local(n):
-        src = eof_ref.at[:, :, pl.ds(pl.multiple_of(n * width, width), width)]
-        return pltpu.make_async_copy(src, eof_buf.at[n, :, pl.ds(0, depth)], eof_lsem.at[n])
-
-    def eof_remote(n):
-        src = eof_ref.at[:, :, pl.ds(pl.multiple_of(n * width, width), width)]
+    def eof_local(n, x):
+        src = eof_ref.at[x, :, pl.ds(pl.multiple_of(n * width, width), width)]
+        return pltpu.make_async_copy(src, eof_buf.at[n, x, pl.ds(0, depth)], eof_lsem.at[x, n])
+
+    def eof_remote(n, x):
+        src = eof_ref.at[x, :, pl.ds(pl.multiple_of(n * width, width), width)]
         return pltpu.make_async_remote_copy(
             src_ref=src,
-            dst_ref=eof_buf.at[n, :, pl.ds(depth, depth)],
-            send_sem=eof_ssem.at[n],
-            recv_sem=eof_rsem.at[n],
+            dst_ref=eof_buf.at[n, x, pl.ds(depth, depth)],
+            send_sem=eof_ssem.at[x, n],
+            recv_sem=eof_rsem.at[x, n],
             device_id=(partner, tile),
             device_id_type=MESH,
         )
@@ -113,7 +113,9 @@
             for q, ref in enumerate((vort_ref, div_ref))
         ]
 
-    lax.fori_loop(0, chunks, lambda n, c: (eof_local(n).start(), c)[1], 0)
+    lax.fori_loop(
+        0, chunks, lambda n, c: (eof_local(n, 0).start(), eof_local(n, 1).start(), c)[2], 0
+    )
 
     barrier = pltpu.get_barrier_semaphore()
     for step in range(1, n_tm):
@@ -144,7 +146,9 @@
         )
         copy.start()
         pcs_copies.append(copy)
-    lax.fori_loop(0, chunks, lambda n, c: (eof_remote(n).start(), c)[1], 0)
+    lax.fori_loop(
+        0, chunks, lambda n, c: (eof_remote(n, 0).start(), eof_remote(n, 1).start(), c)[2], 0
+    )
 
     lag_pad = st_buf.shape[1]
     if lag_pad > lags:
@@ -219,9 +223,9 @@
     build_mix(0, cross)
 
     def send_part(n, carry):
-        eof_local(n).wait()
-        eof_remote(n).wait_recv()
         for x in range(2):
+            eof_local(n, x).wait()
+            eof_remote(n, x).wait_recv()
             send_buf[n, x] = jnp.dot(
                 mix[0], eof_buf[n, x], preferred_element_type=F32
             ).astype(BF16)
@@ -337,8 +341,8 @@
     lax.fori_loop(0, chunks + 2, finish, 0)
 
     def drain(n, carry):
-        eof_remote(n).wait_send()
         for x in range(2):
+            eof_remote(n, x).wait_send()
             part_copy(n, x).wait_send()
 
         @pl.when(has_low)
@@ -392,9 +396,9 @@
             dma,
             dma((n_tm - 1,)),
             dma((n_tm - 1,)),
-            dma((chunks,)),
-            dma((chunks,)),
-            dma((chunks,)),
+            dma((2, chunks)),
+            dma((2, chunks)),
+            dma((2, chunks)),
             dma((2, chunks)),
             dma((2, chunks)),
             dma((2, chunks)),

time: 118 us -> 118 us (level)
  no operation moved by 1% of the time
where the time goes in v4:
time: 118 us
  Pallas kernels  111 us (94%)
  local copies, waits for them, and re-layouts  6.87 us (6%)
    pallas_call x1, Pallas kernels, shards(): pl.pallas_call(functools.partial(kernel, dims), out_shape=[jax.ShapeDtype...  111 us
    unnamed x4, local copies, waits for them, and re-layouts  6.87 us

profile of v4, /device:TPU:0, one launch (start us, length us, event | category | flops | bytes accessed | tf_op | source)
XLA Modules:
  0.0 118.1 jit_solution(15644021869066716967)
XLA Ops:
  0.6 110.6 %reconstruct.1 = (f32[512,2048]{1,0:T(8,128)}, f32[512,2048]{1,0:T(8,128)}) custom-call(f32[2,64]{1,0:T(2,128)} %pcs_ref.1, f32[2,120,512]{2,1,0:T(8,128)} %st_ref.1, bf16[2,1024,2048]{2,1,0:T(8,128)(2,1)} %bitcast.3, s32[8,2048]{1,0:T(8,128)} %mask_ref.1), custom_call_target="tpu_custom_call" | custom-call | tf_op jit(solution)/shard_map/reconstruct/pallas_call | solution.py:379
  111.2 0.0 copy-start
  111.2 4.8 %copy.8 = f32[64,8,2048]{2,1,0:T(8,128)} copy(f32[64,8,2048]{2,1,0:T(8,128)} %bitcast.5) | data formatting | bytes 8388608
  116.1 0.0 copy-done
  116.1 2.0 %copy.9 = f32[64,8,2048]{2,1,0:T(8,128)} copy(f32[64,8,2048]{2,1,0:T(8,128)S(1)} %bitcast.4) | data formatting | bytes 8388608
Async XLA Ops:
  111.2 4.9 %copy-start = (f32[512,2048]{1,0:T(8,128)S(1)}, f32[512,2048]{1,0:T(8,128)}, u32[]{:S(2)}) copy-start(f32[512,2048]{1,0:T(8,128)} %get-tuple-element.5) | copy-start | bytes 12582916
